TPU v7x, 32 devices: a whole 2x2x4 slice. The times are simulated.
32 devices in a mesh: dp: 8 (over z, x), seq: 4 (over y, core).
Axes of the slice: x: 2, y: 2, z: 4, core: 2. Of those that a mesh axis runs over, the one named last changes fastest.
Arguments:
- tokens: bfloat16 [16384, 1024], P(('dp', 'seq')), may hold values from -6 to 6
- time_embed: bfloat16 [32, 1024], P(('dp', 'seq')), may hold values from -6 to 6
- lengths: int32 [32], P('dp'), may hold values from 0 to 475, as said below
- cotangent: bfloat16 [16384, 1024], P(('dp', 'seq')), may hold values from -6 to 6
- w_query: bfloat16 [1024, 1024], P('seq'), may hold values from -0.1875 to 0.1875
- w_key: bfloat16 [1024, 1024], P('seq'), may hold values from -0.1875 to 0.1875
- w_value: bfloat16 [1024, 1024], P('seq'), may hold values from -0.1875 to 0.1875
- w_out: bfloat16 [1024, 1024], P('seq'), may hold values from -0.75 to 0.75
- w_time: bfloat16 [1024, 1024], P('seq'), may hold values from -0.1875 to 0.1875
- w_in: bfloat16 [4096, 1024], P('seq'), may hold values from -0.1875 to 0.1875
- w_down: bfloat16 [4096, 1024], P('seq'), may hold values from -0.09375 to 0.09375
- b_query: bfloat16 [1024], replicated, may hold values from -3 to 3
- b_value: bfloat16 [1024], replicated, may hold values from -3 to 3
- b_out: bfloat16 [1024], replicated, may hold values from -3 to 3
- b_time: bfloat16 [1024], replicated, may hold values from -3 to 3
- b_in: bfloat16 [4096], replicated, may hold values from -3 to 3
- b_down: bfloat16 [1024], replicated, may hold values from -2 to 2
- gain_one: bfloat16 [1024], replicated, may hold values from 0.25 to 1.75
- shift_one: bfloat16 [1024], replicated, may hold values from -2 to 2
- gain_two: bfloat16 [1024], replicated, may hold values from 0.25 to 1.75
- shift_two: bfloat16 [1024], replicated, may hold values from -2 to 2
Outputs:
- layer_out: bfloat16 [16384, 1024], P(('dp', 'seq'))
- grad_tokens: bfloat16 [16384, 1024], P(('dp', 'seq'))
- grad_w_query: float32 [1024, 1024], P('seq')
- grad_w_key: float32 [1024, 1024], P('seq')
- grad_w_value: float32 [1024, 1024], P('seq')
- grad_w_out: float32 [1024, 1024], P('seq')
- grad_w_time: float32 [1024, 1024], P('seq')
- grad_w_in: float32 [4096, 1024], P('seq')
- grad_w_down: float32 [4096, 1024], P('seq')
- grad_b_query: float32 [1024], replicated
- grad_b_value: float32 [1024], replicated
- grad_b_out: float32 [1024], replicated
- grad_b_time: float32 [1024], replicated
- grad_b_in: float32 [4096], replicated
- grad_b_down: float32 [1024], replicated
- grad_gain_one: float32 [1024], replicated
- grad_shift_one: float32 [1024], replicated
- grad_gain_two: float32 [1024], replicated
- grad_shift_two: float32 [1024], replicated
Inputs may be any that keep to these rules, and one draw needn't show every extreme that they name: Item i's valid slots are its first lengths[i] + 25; every draw has an item of length 475 and one of length 0.
All inputs are finite; a program needn't handle non-finite values.
Results may differ from a plain program's by a relative error of at most 0.02.
Values may be sent and summed in bfloat16 or wider, within the bound.
A program may use at most 256 MiB of HBM per device.

v0:
```python
import jax
import jax.numpy as jnp
from jax import lax
from jax.sharding import PartitionSpec as P

HEAD_DIM = 64
BLOCK = 25
norm_eps = 1e-05
neg_large = -1e30


def layer_norm(values, gain, shift):
    center = values - jnp.mean(values, axis=-1, keepdims=True)
    spread = lax.rsqrt(jnp.mean(center * center, axis=-1, keepdims=True) + norm_eps)
    return center * spread * gain + shift


def exact_gelu(values):
    return jax.nn.gelu(values, approximate=False)


def split_heads(rows):
    return rows.reshape(rows.shape[0], rows.shape[1] // HEAD_DIM, HEAD_DIM)


def item_scores(queries, keys, key_valid):
    scores = jnp.einsum(
        "qhd,khd->hqk", split_heads(queries), split_heads(keys), preferred_element_type=jnp.float32
    ) * HEAD_DIM ** (-0.5)
    return jnp.where(key_valid[None, None, :], scores, neg_large)


def attend_forward(queries, keys, values, key_valid):
    masked = item_scores(queries, keys, key_valid)
    row_max = jnp.max(masked, axis=-1, keepdims=True)
    exp_scores = jnp.exp(masked - row_max)
    row_total = jnp.sum(exp_scores, axis=-1, keepdims=True)
    soft = (exp_scores / row_total).astype(jnp.bfloat16)
    mixed = jnp.einsum(
        "hqk,khd->qhd", soft, split_heads(values), preferred_element_type=jnp.float32
    )
    log_total = row_max[:, :, 0] + jnp.log(row_total[:, :, 0])
    return (mixed.reshape(queries.shape).astype(jnp.bfloat16), log_total)


def attend_backward(queries, keys, values, key_valid, log_total, grad_mixed):
    masked = item_scores(queries, keys, key_valid)
    soft = jnp.exp(masked - log_total[:, :, None])
    grad_heads = split_heads(grad_mixed)
    grad_value = jnp.einsum(
        "hqk,qhd->khd", soft.astype(jnp.bfloat16), grad_heads, preferred_element_type=jnp.float32
    )
    grad_soft = jnp.einsum(
        "qhd,khd->hqk", grad_heads, split_heads(values), preferred_element_type=jnp.float32
    )
    grad_scores = soft * (grad_soft - jnp.sum(soft * grad_soft, axis=-1, keepdims=True))
    scores_low = grad_scores.astype(jnp.bfloat16)
    scale = HEAD_DIM ** (-0.5)
    grad_query = scale * jnp.einsum(
        "hqk,khd->qhd", scores_low, split_heads(keys), preferred_element_type=jnp.float32
    )
    grad_key = scale * jnp.einsum(
        "hqk,qhd->khd", scores_low, split_heads(queries), preferred_element_type=jnp.float32
    )
    return tuple(
        (
            grad.reshape(queries.shape).astype(jnp.bfloat16)
            for grad in (grad_query, grad_key, grad_value)
        )
    )


def per_item(fn, item_count, slot_count, *arrays):
    if item_count == 1:
        return fn(*[a[0] for a in arrays])
    outs = lax.map(lambda packed: fn(*packed), arrays)
    return outs


def local(
    tokens,
    time_embed,
    lengths,
    cotangent,
    w_query,
    w_key,
    w_value,
    w_out,
    w_time,
    w_in,
    w_down,
    b_query,
    b_value,
    b_out,
    b_time,
    b_in,
    b_down,
    gain_one,
    shift_one,
    gain_two,
    shift_two,
):
    f32, bf16 = (jnp.float32, jnp.bfloat16)
    seq_rank = lax.axis_index("seq")
    item_count = time_embed.shape[0]
    token_count = tokens.shape[0]
    slot_count = token_count // item_count
    width = tokens.shape[1]
    rows = w_time.shape[0]

    def mm(a, b, dims):
        return lax.dot_general(a, b, (dims, ((), ())), preferred_element_type=f32)

    def gather(a):
        return lax.all_gather(a, "seq", axis=0, tiled=True)

    def scatter_sum(a):
        return lax.psum_scatter(a, "seq", scatter_dimension=0, tiled=True)

    full_time, full_query, full_key, full_value, full_out = (
        gather(w_time),
        gather(w_query),
        gather(w_key),
        gather(w_value),
        gather(w_out),
    )
    own_lengths = lax.dynamic_slice_in_dim(lengths, seq_rank * item_count, item_count, 0)
    slot_index = lax.broadcasted_iota(jnp.int32, (item_count, slot_count), 1)
    own_valid = slot_index < own_lengths[:, None] + BLOCK
    row_keep = own_valid.reshape(token_count, 1).astype(f32)
    time_proj = mm(time_embed, full_time, ((1,), (0,))) + b_time.astype(f32)
    resid = (tokens.reshape(item_count, slot_count, width) + time_proj[:, None, :]).reshape(
        token_count, width
    )
    resid_low = resid.astype(bf16)
    query_rows = (mm(resid_low, full_query, ((1,), (0,))) + b_query.astype(f32)).astype(bf16)
    key_rows = mm(resid_low, full_key, ((1,), (0,))).astype(bf16)
    value_rows = (mm(resid_low, full_value, ((1,), (0,))) + b_value.astype(f32)).astype(bf16)

    def split_items(a):
        return a.reshape(item_count, slot_count, -1)

    qkv = [split_items(a) for a in (query_rows, key_rows, value_rows)]
    mixed, log_total = per_item(attend_forward, item_count, slot_count, *qkv, own_valid)
    mixed_rows = mixed.reshape(token_count, width)
    attn_out = mm(mixed_rows, full_out, ((1,), (0,))) + b_out.astype(f32)
    first_norm, first_pull = jax.vjp(
        layer_norm, resid + attn_out, gain_one.astype(f32), shift_one.astype(f32)
    )
    first_group = gather(first_norm.astype(bf16))
    bias_in = lax.dynamic_slice_in_dim(b_in, seq_rank * w_in.shape[0], w_in.shape[0], 0)
    hidden_pre = mm(first_group, w_in, ((1,), (1,))) + bias_in.astype(f32)
    hidden, gelu_pull = jax.vjp(exact_gelu, hidden_pre)
    hidden_low = hidden.astype(bf16)
    ffn_part = mm(hidden_low, w_down, ((1,), (0,))).astype(bf16)
    ffn_out = scatter_sum(ffn_part).astype(f32) + b_down.astype(f32)
    second_norm, second_pull = jax.vjp(
        layer_norm, first_norm + ffn_out, gain_two.astype(f32), shift_two.astype(f32)
    )
    layer_out = (second_norm * row_keep).astype(bf16)
    grad_second_in, grad_gain_two, grad_shift_two = second_pull(cotangent.astype(f32) * row_keep)
    grad_ffn = grad_second_in.astype(bf16)
    grad_group = gather(grad_ffn)
    grad_hidden = mm(grad_group, w_down, ((1,), (1,)))
    grad_pre = gelu_pull(grad_hidden)[0].astype(bf16)
    back_part = mm(grad_pre, w_in, ((1,), (0,))).astype(bf16)
    grad_first = grad_second_in + scatter_sum(back_part).astype(f32)
    term_in = mm(grad_pre, first_group, ((0,), (0,))).astype(bf16)
    term_down = mm(hidden_low, grad_group, ((0,), (0,))).astype(bf16)
    sum_ffn = lax.psum(jnp.concatenate([term_in, term_down], axis=0), "dp").astype(f32)
    grad_first_in, grad_gain_one, grad_shift_one = first_pull(grad_first)
    grad_attn = grad_first_in.astype(bf16)
    grad_mixed = mm(grad_attn, full_out, ((1,), (1,))).astype(bf16)
    if item_count == 1:
        extra = (log_total[None], split_items(grad_mixed))
    else:
        extra = (log_total, split_items(grad_mixed))
    grad_query, grad_key, grad_value = (
        a.reshape(token_count, width)
        for a in per_item(attend_backward, item_count, slot_count, *qkv, own_valid, *extra)
    )
    grad_resid = (
        grad_first_in
        + mm(grad_query, full_query, ((1,), (1,)))
        + mm(grad_key, full_key, ((1,), (1,)))
        + mm(grad_value, full_value, ((1,), (1,)))
    )
    grad_tokens = grad_resid.astype(bf16)
    grad_time = jnp.sum(grad_resid.reshape(item_count, slot_count, width), axis=1).astype(bf16)
    terms = [
        mm(resid_low, grad_query, ((0,), (0,))),
        mm(resid_low, grad_key, ((0,), (0,))),
        mm(resid_low, grad_value, ((0,), (0,))),
        mm(mixed_rows, grad_attn, ((0,), (0,))),
    ]
    group = w_out.shape[0]
    stacked = jnp.stack([t.astype(bf16).reshape(-1, group, width) for t in terms], axis=1)
    share = scatter_sum(stacked.reshape(-1, width))
    sum_attn = lax.psum(share, "dp").astype(f32)
    small = jnp.concatenate(
        [
            jnp.stack(
                [
                    jnp.sum(grad_query, axis=0, dtype=f32),
                    jnp.sum(grad_value, axis=0, dtype=f32),
                    jnp.sum(grad_attn, axis=0, dtype=f32),
                    jnp.sum(grad_ffn, axis=0, dtype=f32),
                    grad_gain_one,
                    grad_shift_one,
                    grad_gain_two,
                    grad_shift_two,
                ]
            ).astype(bf16),
            jnp.sum(grad_pre, axis=0, dtype=f32).reshape(-1, width).astype(bf16),
            time_embed,
            grad_time,
        ],
        axis=0,
    )
    every = lax.all_gather(small, ("dp", "seq"), axis=0)
    vectors = jnp.sum(every[:, :8], axis=0, dtype=f32)
    hidden_rows = every.shape[1] - 8 - 2 * item_count
    in_parts = every[:, 8 : 8 + hidden_rows].reshape(-1, b_in.shape[0])
    grad_b_in = jnp.sum(in_parts, axis=0, dtype=f32)
    time_rows = every[:, 8 + hidden_rows : 8 + hidden_rows + item_count].reshape(-1, width)
    time_grads = every[:, 8 + hidden_rows + item_count :].reshape(-1, width)
    own_columns = lax.dynamic_slice_in_dim(time_rows, seq_rank * rows, rows, 1)
    grad_w_time = mm(own_columns, time_grads, ((0,), (0,)))
    grad_b_time = jnp.sum(time_grads, axis=0, dtype=f32)
    return (
        layer_out,
        grad_tokens,
        sum_attn[:group],
        sum_attn[group : 2 * group],
        sum_attn[2 * group : 3 * group],
        sum_attn[3 * group :],
        grad_w_time,
        sum_ffn[: w_in.shape[0]],
        sum_ffn[w_in.shape[0] :],
        vectors[0],
        vectors[1],
        vectors[2],
        grad_b_time,
        grad_b_in,
        vectors[3],
        vectors[4],
        vectors[5],
        vectors[6],
        vectors[7],
    )


def solution(mesh):
    in_specs = (
        P(("dp", "seq"), None),
        P(("dp", "seq"), None),
        P("dp"),
        P(("dp", "seq"), None),
        P("seq", None),
        P("seq", None),
        P("seq", None),
        P("seq", None),
        P("seq", None),
        P("seq", None),
        P("seq", None),
        P(),
        P(),
        P(),
        P(),
        P(),
        P(),
        P(),
        P(),
        P(),
        P(),
    )
    out_specs = (
        P(("dp", "seq"), None),
        P(("dp", "seq"), None),
        P("seq", None),
        P("seq", None),
        P("seq", None),
        P("seq", None),
        P("seq", None),
        P("seq", None),
        P("seq", None),
        P(),
        P(),
        P(),
        P(),
        P(),
        P(),
        P(),
        P(),
        P(),
        P(),
    )
    return jax.shard_map(local, mesh=mesh, in_specs=in_specs, out_specs=out_specs, check_vma=False)
```

profile of v0, /device:TPU:0, one launch (start us, length us, event | category | flops | bytes accessed | tf_op | source)
XLA Modules:
  0.0 732.2 jit_solution(3286179977434555433)
XLA Ops:
  16.0 18.9 %all-gather.10.cloned.1.call-done = bf16[1024,1024]{1,0:T(8,128)(2,1)} async-done(((bf16[256,1024]{1,0:T(8,128)(2,1)}), bf16[1024,1024]{1,0:T(8,128)(2,1)}) %all-gather.10.cloned.1.call-update) | async-done | bytes 2097168 | tf_op jit(solution)/shard_map/all_gather | solution.py:115
  34.9 2.0 fusion.28
  36.9 22.1 %all-gather.14.cloned.1.call-done = bf16[1024,1024]{1,0:T(8,128)(2,1)} async-done(((bf16[256,1024]{1,0:T(8,128)(2,1)}), bf16[1024,1024]{1,0:T(8,128)(2,1)}) %all-gather.14.cloned.1.call-update) | async-done | bytes 2097168 | tf_op jit(solution)/shard_map/all_gather | solution.py:115
  59.1 3.2 add_convert_fusion.1
  62.2 1.3 copy.72
  63.6 19.7 %all-gather.16.cloned.1.call-done = bf16[1024,1024]{1,0:T(8,128)(2,1)} async-done(((bf16[256,1024]{1,0:T(8,128)(2,1)}), bf16[1024,1024]{1,0:T(8,128)(2,1)}) %all-gather.16.cloned.1.call-update) | async-done | bytes 2097168 | tf_op jit(solution)/shard_map/all_gather | solution.py:115
  83.2 4.1 convolution_convert_fusion.9
  87.4 1.5 copy.73
  88.9 9.2 %fusion.46 = (f32[16,512]{1,0:T(8,128)S(1)}, f32[16,512,512]{1,2,0:T(8,128)}) fusion(bf16[512,16,64]{0,2,1:T(8,128)(2,1)} %bitcast.89, bf16[512,16,64]{0,2,1:T(8,128)(2,1)S(1)} %bitcast.87, pred[512]{0:T(512)(128)(4,1)S(1)} %iota_compare_fusion), kind=kOutput, calls=%fused_computation.107 | convolution fusion | flops 549445632 | bytes 18907648 | tf_op jit(solution)/shard_map/qhd,khd->hqk/dot_general | solution.py:27
  98.0 9.2 %all-gather.12.cloned.1.call-done = bf16[1024,1024]{1,0:T(8,128)(2,1)} async-done(((bf16[256,1024]{1,0:T(8,128)(2,1)}), bf16[1024,1024]{1,0:T(8,128)(2,1)}) %all-gather.12.cloned.1.call-update) | async-done | bytes 2097168 | tf_op jit(solution)/shard_map/all_gather | solution.py:115
  107.2 4.1 add_convert_fusion.2
  111.4 1.5 copy.71
  112.9 9.4 %fusion = f32[16,512]{1,0:T(8,128)S(1)} fusion(f32[16,512,512]{1,2,0:T(8,128)} %get-tuple-element.61, f32[16,512]{1,0:T(8,128)S(1)} %get-tuple-element.60), kind=kLoop, calls=%fused_computation.6 | loop fusion | flops 8380416 | bytes 16842752 | tf_op jit(solution)/shard_map/reduce_sum | solution.py:37
  122.2 8.5 %fusion.16 = bf16[16,64,512]{2,1,0:T(8,128)(2,1)} fusion(bf16[512,16,64]{0,2,1:T(8,128)(2,1)S(1)} %bitcast.93, f32[16,512,512]{1,2,0:T(8,128)} %get-tuple-element.61, f32[16,512]{1,0:T(8,128)S(1)} %fusion, f32[16,512]{1,0:T(8,128)S(1)} %get-tuple-element.60), kind=kOutput, calls=%fused_computation.64 | convolution fusion | flops 549978112 | bytes 18939904 | tf_op jit(solution)/shard_map/hqk,khd->qhd/dot_general | solution.py:39
  131.2 3.6 fusion.47
  136.1 1.4 fusion.15
  138.5 33.7 %all-gather.20.cloned.1.call-done = bf16[2048,1024]{1,0:T(8,128)(2,1)} async-done(((bf16[512,1024]{1,0:T(8,128)(2,1)}), bf16[2048,1024]{1,0:T(8,128)(2,1)}) %all-gather.20.cloned.1.call-update) | async-done | bytes 4194320 | tf_op jit(solution)/shard_map/all_gather | solution.py:115
  172.1 25.7 %multiply_convert_fusion.1 = (bf16[2048,1024]{1,0:T(8,128)(2,1)S(1)}, f32[2048,1024]{1,0:T(8,128)}, f32[2048,1024]{1,0:T(8,128)}) fusion(f32[1024]{0:T(1024)S(1)} %dynamic-slice_convert_fusion, bf16[2048,1024]{1,0:T(8,128)(2,1)} %all-gather.20.cloned.1.call-done, bf16[1024,1024]{1,0:T(8,128)(2,1)S(1)} %copy-done), kind=kOutput, calls=%fused_computation.14 | convolution fusion | flops 4433379328 | bytes 27267072 | tf_op jit(solution)/shard_map/dot_general | solution.py:112
  197.8 2.0 copy-done.36
  199.8 6.0 convolution_convert_fusion.1
  206.6 44.0 %reduce-scatter.4.cloned.1.call-done = bf16[512,1024]{1,0:T(8,128)(2,1)} async-done(((bf16[2048,1024]{1,0:T(8,128)(2,1)}), bf16[512,1024]{1,0:T(8,128)(2,1)}) %reduce-scatter.4.cloned.1.call-update) | async-done | bytes 1048592 | tf_op jit(solution)/shard_map/reduce_scatter | solution.py:118
  250.6 2.7 fusion.39
  254.6 2.0 fusion.38
  259.6 34.2 %all-gather.22.cloned.1.call-done = bf16[2048,1024]{1,0:T(8,128)(2,1)} async-done(((bf16[512,1024]{1,0:T(8,128)(2,1)}), bf16[2048,1024]{1,0:T(8,128)(2,1)}) %all-gather.22.cloned.1.call-update) | async-done | bytes 4194320 | tf_op jit(solution)/shard_map/all_gather | solution.py:115
  293.8 13.3 %fusion.34 = (bf16[1024]{0:T(1024)(128)(2,1)S(1)}, bf16[2048,1024]{1,0:T(8,128)(2,1)S(1)}) fusion(f32[2048,1024]{1,0:T(8,128)} %get-tuple-element.40, f32[2048,1024]{1,0:T(8,128)} %get-tuple-element.64, f32[1024]{0:T(1024)S(1)} %dynamic-slice_convert_fusion, bf16[2048,1024]{1,0:T(8,128)(2,1)} %all-gather.22.cloned.1.call-done, bf16[1024,1024]{1,0:T(8,128)(2,1)} %param.31), kind=kOutput, calls=%fused_computation.96 | convolution fusion | flops 4328520704 | bytes 27269120 | tf_op jit(solution)/shard_map/dot_general | solution.py:112
  307.2 1.9 copy-done.37
  309.1 6.0 convolution_convert_fusion
  315.2 44.7 %reduce-scatter.6.cloned.1.call-done = bf16[512,1024]{1,0:T(8,128)(2,1)} async-done(((bf16[2048,1024]{1,0:T(8,128)(2,1)}), bf16[512,1024]{1,0:T(8,128)(2,1)}) %reduce-scatter.6.cloned.1.call-update) | async-done | bytes 1048592 | tf_op jit(solution)/shard_map/reduce_scatter | solution.py:118
  359.8 3.7 multiply_reduce_fusion.2
  366.5 2.3 convolution_convert_fusion.8
  368.7 1.5 copy.75
  370.2 11.4 %multiply_reduce_fusion = (f32[16,512]{1,0:T(8,128)S(1)}, f32[16,512,512]{1,2,0:T(8,128)}) fusion(f32[16,512,512]{1,2,0:T(8,128)} %get-tuple-element.61, f32[16,512]{1,0:T(8,128)S(1)} %log_add_fusion, bf16[512,16,64]{0,2,1:T(8,128)(2,1)S(1)} %bitcast.91, bf16[512,16,64]{0,2,1:T(8,128)(2,1)} %bitcast.94), kind=kOutput, calls=%fused_computation.1 | convolution fusion | flops 549445632 | bytes 35717120 | tf_op jit(solution)/shard_map/qhd,khd->hqk/dot_general | solution.py:53
  381.6 12.0 %multiply_convert_fusion = bf16[16,512,512]{1,2,0:T(8,128)(2,1)S(1)} fusion(f32[16,512,512]{1,2,0:T(8,128)} %get-tuple-element.66, f32[16,512,512]{1,2,0:T(8,128)} %get-tuple-element.61, f32[16,512]{1,0:T(8,128)S(1)} %get-tuple-element.65, f32[16,512]{1,0:T(8,128)S(1)} %log_add_fusion), kind=kLoop, calls=%fused_computation | loop fusion | flops 16777216 | bytes 42008576 | tf_op jit(solution)/shard_map/convert_element_type | solution.py:57
  393.6 1.5 bitcast_reduce_fusion.1
  395.2 2.6 multiply_convert_fusion.2
  399.1 8.6 %bitcast_reduce_fusion = (bf16[16,64]{1,0:T(8,128)(2,1)S(1)}, bf16[16,64,512]{2,1,0:T(8,128)(2,1)S(1)}) fusion(bf16[512,16,64]{0,2,1:T(8,128)(2,1)S(1)} %bitcast.92, f32[16,512,512]{1,2,0:T(8,128)} %get-tuple-element.61, f32[16,512]{1,0:T(8,128)S(1)} %log_add_fusion), kind=kOutput, calls=%fused_computation.68 | convolution fusion | flops 546307072 | bytes 18909184 | tf_op jit(solution)/shard_map/hqk,qhd->khd/dot_general | solution.py:50
  411.8 3.8 pad_maximum_fusion
  415.6 7.9 %copy.79 = bf16[4,4,256,1024]{3,2,1,0:T(8,128)(2,1)} copy(bf16[4,4,256,1024]{3,2,0,1:T(8,128)(2,1)} %pad_maximum_fusion) | data formatting | bytes 16777216 | tf_op jit(solution)/shard_map/stack | solution.py:197
  423.9 8.2 %convolution_convert_fusion.2 = bf16[1024,1024]{1,0:T(8,128)(2,1)S(1)} fusion(bf16[2048,1024]{1,0:T(8,128)(2,1)} %copy-done.36, bf16[2048,1024]{1,0:T(8,128)(2,1)} %all-gather.22.cloned.1.call-done), kind=kOutput, calls=%fused_computation.57 | convolution fusion | flops 4296015872 | bytes 10485760 | tf_op jit(solution)/shard_map/dot_general | solution.py:112
  432.1 4.8 convolution_convert_fusion.3
  436.9 2.5 pad_maximum_fusion.1
  439.3 55.8 %reduce-scatter.8.cloned.1.call-done = bf16[1024,1024]{1,0:T(8,128)(2,1)} async-done(((bf16[4096,1024]{1,0:T(8,128)(2,1)}), bf16[1024,1024]{1,0:T(8,128)(2,1)}) %reduce-scatter.8.cloned.1.call-update) | async-done | bytes 2097168 | tf_op jit(solution)/shard_map/reduce_scatter | solution.py:118
  495.2 3.0 fusion.48
  500.8 2.5 fusion.42
  503.7 51.7 %all-gather.1 = bf16[32,11,1024]{2,1,0:T(8,128)(2,1)S(1)} all-gather(bf16[1,11,1024]{2,1,0:T(8,128)(2,1)S(1)} %bitcast.107), channel_id=2, replica_groups=mesh['dp'=8,'seq'=4] {'dp','seq'}, dimensions={0}, use_global_device_ids=true | all-gather | bytes 743424 | tf_op jit(solution)/shard_map/all_gather | solution.py:220
  559.3 156.8 %all-reduce.3.cloned.1.call-done = (bf16[1024,1024]{1,0:T(8,128)(2,1)}, bf16[2048,1024]{1,0:T(8,128)(2,1)}) async-done(((bf16[1024,1024]{1,0:T(8,128)(2,1)}, bf16[2048,1024]{1,0:T(8,128)(2,1)}), (bf16[1024,1024]{1,0:T(8,128)(2,1)}, bf16[2048,1024]{1,0:T(8,128)(2,1)})) %all-reduce.3.cloned.1.call-update) | async-done | bytes 6291472 | tf_op jit(solution)/shard_map/psum | solution.py:199
  716.2 6.8 fusion.41
  723.0 2.2 fusion.43
  (152 shorter events, 31.1 us)
Async XLA Ops:
  7.2 164.9 %copy-start = (bf16[1024,1024]{1,0:T(8,128)(2,1)S(1)}, bf16[1024,1024]{1,0:T(8,128)(2,1)}, u32[]{:S(2)}) copy-start(bf16[1024,1024]{1,0:T(8,128)(2,1)} %param.30) | copy-start | bytes 6291460
  7.2 29.7 %copy-start.28 = (bf16[1024]{0:T(1024)(128)(2,1)S(1)}, bf16[1024]{0:T(1024)(128)(2,1)}, u32[]{:S(2)}) copy-start(bf16[1024]{0:T(1024)(128)(2,1)} %param.35) | copy-start | bytes 6148
  7.2 27.7 %all-gather.10.cloned.1.call-start = ((), (), s32[]{:S(2)}) async-start(), calls=%async_computation.3 | async-start | bytes 2621440 | tf_op jit(solution)/shard_map/all_gather | solution.py:115
  7.9 51.1 %all-gather.14.cloned.1.call-start = ((), (), s32[]{:S(2)}) async-start(), calls=%async_computation.5 | async-start | bytes 2621440 | tf_op jit(solution)/shard_map/all_gather | solution.py:115
  8.7 74.5 %all-gather.16.cloned.1.call-start = ((), (), s32[]{:S(2)}) async-start(), calls=%async_computation.6 | async-start | bytes 2621440 | tf_op jit(solution)/shard_map/all_gather | solution.py:115
  9.4 97.8 %all-gather.12.cloned.1.call-start = ((), (), s32[]{:S(2)}) async-start(), calls=%async_computation.4 | async-start | bytes 2621440 | tf_op jit(solution)/shard_map/all_gather | solution.py:115
  10.0 121.2 %all-gather.18.cloned.1.call-start = ((), (), s32[]{:S(2)}) async-start(), calls=%async_computation.7 | async-start | bytes 2621440 | tf_op jit(solution)/shard_map/all_gather | solution.py:115
  10.6 161.5 %all-gather.20.cloned.1.call-start = ((), (), s32[]{:S(2)}) async-start(), calls=%async_computation.8 | async-start | bytes 5242880 | tf_op jit(solution)/shard_map/all_gather | solution.py:115
  36.9 94.3 %copy-start.25 = (f32[1024]{0:T(1024)}, f32[1024]{0:T(1024)S(1)}, u32[]{:S(2)}) copy-start(f32[1024]{0:T(1024)S(1)} %convert_add_fusion.2) | copy-start | bytes 12292
  88.9 9.2 %copy-start.5 = (bf16[512,1024]{0,1:T(8,128)(2,1)}, bf16[512,1024]{0,1:T(8,128)(2,1)S(1)}, u32[]{:S(2)}) copy-start(bf16[512,1024]{0,1:T(8,128)(2,1)S(1)} %copy.73) | copy-start | bytes 3145732
  112.9 9.4 %copy-start.11 = (bf16[512,1024]{0,1:T(8,128)(2,1)}, bf16[512,1024]{0,1:T(8,128)(2,1)S(1)}, u32[]{:S(2)}) copy-start(bf16[512,1024]{0,1:T(8,128)(2,1)S(1)} %copy.71) | copy-start | bytes 3145732
  134.8 1.3 copy-start.1
  137.5 113.1 %reduce-scatter.4.cloned.1.call-start = ((), (), s32[]{:S(2)}) async-start(), calls=%async_computation.9 | async-start | bytes 5242880 | tf_op jit(solution)/shard_map/reduce_scatter | solution.py:118
  172.1 27.7 %copy-start.33 = (bf16[1024,1024]{1,0:T(8,128)(2,1)S(1)}, bf16[1024,1024]{1,0:T(8,128)(2,1)}, u32[]{:S(2)}) copy-start(bf16[1024,1024]{1,0:T(8,128)(2,1)} %param.31) | copy-start | bytes 6291460
  197.8 2.0 copy-start.36
  205.8 0.7 copy-start.31
  205.9 47.8 %copy-start.12 = (bf16[512,1024]{1,0:T(8,128)(2,1)S(1)}, bf16[512,1024]{1,0:T(8,128)(2,1)}, u32[]{:S(2)}) copy-start(bf16[512,1024]{1,0:T(8,128)(2,1)} %param.24) | copy-start | bytes 3145732
  205.9 87.9 %all-gather.22.cloned.1.call-start = ((), (), s32[]{:S(2)}) async-start(), calls=%async_computation.10 | async-start | bytes 5242880 | tf_op jit(solution)/shard_map/all_gather | solution.py:115
  256.6 1.3 copy-start.3
  259.2 100.6 %reduce-scatter.6.cloned.1.call-start = ((), (), s32[]{:S(2)}) async-start(), calls=%async_computation.11 | async-start | bytes 5242880 | tf_op jit(solution)/shard_map/reduce_scatter | solution.py:118
  307.1 1.9 copy-start.37
  315.1 180.0 %reduce-scatter.8.cloned.1.call-start = ((), (), s32[]{:S(2)}) async-start(), calls=%async_computation.12 | async-start | bytes 10485760 | tf_op jit(solution)/shard_map/reduce_scatter | solution.py:118
  359.8 3.7 copy-start.2
  359.8 3.8 copy-start.4
  359.8 4.0 copy-start.13
  363.9 2.6 copy-start.16
  364.8 1.3 copy-start.8
  365.1 1.4 copy-start.19
  381.6 12.0 %copy-start.6 = (bf16[512,1024]{0,1:T(8,128)(2,1)S(1)}, bf16[512,1024]{0,1:T(8,128)(2,1)}, u32[]{:S(2)}) copy-start(bf16[512,1024]{0,1:T(8,128)(2,1)} %copy-done.5) | copy-start | bytes 3145732
  393.6 1.5 copy-start.7
  395.2 12.6 %copy-start.14 = (bf16[16,64,512]{2,1,0:T(8,128)(2,1)}, bf16[16,64,512]{2,1,0:T(8,128)(2,1)S(1)}, u32[]{:S(2)}) copy-start(bf16[16,64,512]{2,1,0:T(8,128)(2,1)S(1)} %get-tuple-element.69) | copy-start | bytes 3145732
  395.2 2.7 copy-start.20
  395.2 2.6 copy-start.22
  397.8 11.3 %copy-start.17 = (bf16[16,64,512]{2,1,0:T(8,128)(2,1)}, bf16[16,64,512]{2,1,0:T(8,128)(2,1)S(1)}, u32[]{:S(2)}) copy-start(bf16[16,64,512]{2,1,0:T(8,128)(2,1)S(1)} %multiply_convert_fusion.2) | copy-start | bytes 3145732
  399.1 8.7 %copy-start.21 = (bf16[512,1024]{1,0:T(8,128)(2,1)S(1)}, bf16[512,1024]{1,0:T(8,128)(2,1)}, u32[]{:S(2)}) copy-start(bf16[512,1024]{1,0:T(8,128)(2,1)} %param.21) | copy-start | bytes 3145732
  399.1 8.7 %copy-start.26 = (f32[1024]{0:T(1024)S(1)}, f32[1024]{0:T(1024)}, u32[]{:S(2)}) copy-start(f32[1024]{0:T(1024)} %copy-done.25) | copy-start | bytes 12292
  407.8 2.7 copy-start.23
  423.6 292.6 %all-reduce.3.cloned.1.call-start = ((), (), s32[]{:S(2)}) async-start(), calls=%async_computation.13 | async-start | bytes 12582912 | tf_op jit(solution)/shard_map/psum | solution.py:199
  423.8 8.2 %copy-start.32 = (bf16[2048,1024]{1,0:T(8,128)(2,1)S(1)}, bf16[2048,1024]{1,0:T(8,128)(2,1)}, u32[]{:S(2)}) copy-start(bf16[2048,1024]{1,0:T(8,128)(2,1)} %all-gather.20.cloned.1.call-done) | copy-start | bytes 12582916
  423.8 8.2 %copy-start.38 = (bf16[2048,1024]{1,0:T(8,128)(2,1)S(1)}, bf16[2048,1024]{1,0:T(8,128)(2,1)}, u32[]{:S(2)}) copy-start(bf16[2048,1024]{1,0:T(8,128)(2,1)} %copy-done.37) | copy-start | bytes 12582916
  439.3 55.9 %copy-start.15 = (bf16[16,64,512]{2,1,0:T(8,128)(2,1)S(1)}, bf16[16,64,512]{2,1,0:T(8,128)(2,1)}, u32[]{:S(2)}) copy-start(bf16[16,64,512]{2,1,0:T(8,128)(2,1)} %copy-done.14) | copy-start | bytes 3145732
  495.2 3.1 copy-start.18
  495.2 3.1 copy-start.34
  498.3 1.6 copy-start.9
  498.3 1.8 copy-start.24
  498.3 2.5 copy-start.35
  500.8 2.8 copy-start.27
  716.2 6.8 copy-start.10
  (2 other events, 1.4 us)
Sparse Core Ops, SparseCore 0:
  9.6 25.2 all-gather.9
  36.5 22.5 all-gather.13
  60.6 22.5 all-gather.15
  84.6 22.5 all-gather.11
  108.6 22.5 all-gather.17
  137.6 34.4 all-gather.19
  206.0 44.5 reduce-scatter.3
  259.3 34.4 all-gather.21
  315.2 44.5 reduce-scatter.5
  423.7 71.3 reduce-scatter.7
  499.6 216.4 all-reduce.2
where the time goes:
time: 741 us; the launch traced here: 732 us
  waiting for transfers between devices  443 us (60%)
  matrix products  138 us (19%)
  blocking collectives  51.7 us (7%)
  other arithmetic  47.2 us (6%)
  local copies, waits for them, and re-layouts  35.2 us (5%)
  between operations  15.6 us (2%)
    psum x1, waiting for transfers between devices, local(): sum_attn = lax.psum(share, 'dp').astype(f32)  157 us
    reduce_scatter x3, waiting for transfers between devices, scatter_sum(): return lax.psum_scatter(a, 'seq', scatter_dimension=0, tiled=True)  145 us
    all_gather x7, waiting for transfers between devices, gather(): return lax.all_gather(a, 'seq', axis=0, tiled=True)  138 us
    dot_general x20, matrix products, mm(): return lax.dot_general(a, b, (dims, ((), ())), preferred_element_type=f32)  96.6 us
    all_gather x1, blocking collectives, local(): every = lax.all_gather(small, ('dp', 'seq'), axis=0)  51.7 us
  transfers between devices with their start and end apart: 11, of which 11 were waited for; matrix products, arithmetic and copies ran while one was open for 10% of the time, Pallas kernels for 0%

commit v1 on v0

--- a/solution.py
+++ b/solution.py
@@ -196,7 +196,7 @@
     group = w_out.shape[0]
     stacked = jnp.stack([t.astype(bf16).reshape(-1, group, width) for t in terms], axis=1)
     share = scatter_sum(stacked.reshape(-1, width))
-    sum_attn = lax.psum(share, "dp").astype(f32)
+    sum_attn = jnp.sum(lax.all_gather(share, "dp"), axis=0).astype(f32)
     small = jnp.concatenate(
         [
             jnp.stack(

time: 741 us -> 913 us (1.23)
  waiting for transfers between devices: 443 us -> 612 us
  other arithmetic: 47.2 us -> 58 us
    all_gather x0 -> x1, waiting for transfers between devices: none -> 166 us  [local(): sum_attn = jnp.sum(lax.all_gather(share, 'dp'), axis=0).astype(f32)]
    reduce_sum x0 -> x1, other arithmetic: none -> 10.8 us  [local(): sum_attn = jnp.sum(lax.all_gather(share, 'dp'), axis=0).astype(f32)]
  transfers between devices with their start and end apart: 11 -> 12, of which waited for: 11 -> 12; matrix products, arithmetic and copies ran while one was open for 10% -> 9% of each run, Pallas kernels for 0% -> 0%
where the time goes in v1:
time: 913 us; the launch traced here: 904 us
  waiting for transfers between devices  612 us (67%)
  matrix products  137 us (15%)
  other arithmetic  58 us (6%)
  blocking collectives  49 us (5%)
  local copies, waits for them, and re-layouts  30.8 us (3%)
  between operations  15.9 us (2%)
    all_gather x1, waiting for transfers between devices, local(): sum_attn = jnp.sum(lax.all_gather(share, 'dp'), axis=0).astype(f32)  166 us
    psum x1, waiting for transfers between devices, local(): lax.psum(jnp.concatenate([term_in, term_down], axis=0), 'dp').astype(f32)  161 us
    reduce_scatter x3, waiting for transfers between devices, scatter_sum(): return lax.psum_scatter(a, 'seq', scatter_dimension=0, tiled=True)  144 us
    all_gather x7, waiting for transfers between devices, gather(): return lax.all_gather(a, 'seq', axis=0, tiled=True)  138 us
    dot_general x20, matrix products, mm(): return lax.dot_general(a, b, (dims, ((), ())), preferred_element_type=f32)  94.9 us
    all_gather x1, blocking collectives, local(): every = lax.all_gather(small, ('dp', 'seq'), axis=0)  49 us
  transfers between devices with their start and end apart: 12, of which 12 were waited for; matrix products, arithmetic and copies ran while one was open for 9% of the time, Pallas kernels for 0%

profile of v1, /device:TPU:0, one launch (start us, length us, event | category | flops | bytes accessed | tf_op | source)
XLA Modules:
  0.0 904.0 jit_solution(4009528641068321788)
XLA Ops:
  16.0 18.9 %all-gather.12.cloned.1.call-done = bf16[1024,1024]{1,0:T(8,128)(2,1)} async-done(((bf16[256,1024]{1,0:T(8,128)(2,1)}), bf16[1024,1024]{1,0:T(8,128)(2,1)}) %all-gather.12.cloned.1.call-update) | async-done | bytes 2097168 | tf_op jit(solution)/shard_map/all_gather | solution.py:115
  34.9 2.0 fusion.28
  36.9 22.1 %all-gather.16.cloned.1.call-done = bf16[1024,1024]{1,0:T(8,128)(2,1)} async-done(((bf16[256,1024]{1,0:T(8,128)(2,1)}), bf16[1024,1024]{1,0:T(8,128)(2,1)}) %all-gather.16.cloned.1.call-update) | async-done | bytes 2097168 | tf_op jit(solution)/shard_map/all_gather | solution.py:115
  59.1 3.2 add_convert_fusion.1
  62.2 1.3 copy.77
  63.6 19.7 %all-gather.18.cloned.1.call-done = bf16[1024,1024]{1,0:T(8,128)(2,1)} async-done(((bf16[256,1024]{1,0:T(8,128)(2,1)}), bf16[1024,1024]{1,0:T(8,128)(2,1)}) %all-gather.18.cloned.1.call-update) | async-done | bytes 2097168 | tf_op jit(solution)/shard_map/all_gather | solution.py:115
  83.2 4.1 convolution_convert_fusion.9
  87.4 1.5 copy.78
  88.9 9.2 %fusion.46 = (f32[16,512]{1,0:T(8,128)S(1)}, f32[16,512,512]{1,2,0:T(8,128)}) fusion(bf16[512,16,64]{0,2,1:T(8,128)(2,1)} %bitcast.99, bf16[512,16,64]{0,2,1:T(8,128)(2,1)S(1)} %bitcast.97, pred[512]{0:T(512)(128)(4,1)S(1)} %iota_compare_fusion), kind=kOutput, calls=%fused_computation.107 | convolution fusion | flops 549445632 | bytes 18907648 | tf_op jit(solution)/shard_map/qhd,khd->hqk/dot_general | solution.py:27
  98.1 9.2 %all-gather.14.cloned.1.call-done = bf16[1024,1024]{1,0:T(8,128)(2,1)} async-done(((bf16[256,1024]{1,0:T(8,128)(2,1)}), bf16[1024,1024]{1,0:T(8,128)(2,1)}) %all-gather.14.cloned.1.call-update) | async-done | bytes 2097168 | tf_op jit(solution)/shard_map/all_gather | solution.py:115
  107.2 4.1 add_convert_fusion.2
  111.4 1.5 copy.76
  112.9 9.4 %fusion = f32[16,512]{1,0:T(8,128)S(1)} fusion(f32[16,512,512]{1,2,0:T(8,128)} %get-tuple-element.59, f32[16,512]{1,0:T(8,128)S(1)} %get-tuple-element.58), kind=kLoop, calls=%fused_computation.6 | loop fusion | flops 8380416 | bytes 16842752 | tf_op jit(solution)/shard_map/reduce_sum | solution.py:37
  122.2 8.5 fusion.16
  131.2 3.6 fusion.47
  136.1 1.4 fusion.15
  138.5 33.7 %all-gather.22.cloned.1.call-done = bf16[2048,1024]{1,0:T(8,128)(2,1)} async-done(((bf16[512,1024]{1,0:T(8,128)(2,1)}), bf16[2048,1024]{1,0:T(8,128)(2,1)}) %all-gather.22.cloned.1.call-update) | async-done | bytes 4194320 | tf_op jit(solution)/shard_map/all_gather | solution.py:115
  172.1 25.6 %multiply_convert_fusion.1 = (bf16[2048,1024]{1,0:T(8,128)(2,1)S(1)}, f32[2048,1024]{1,0:T(8,128)}, f32[2048,1024]{1,0:T(8,128)}) fusion(f32[1024]{0:T(1024)S(1)} %dynamic-slice_convert_fusion, bf16[2048,1024]{1,0:T(8,128)(2,1)} %all-gather.22.cloned.1.call-done, bf16[1024,1024]{1,0:T(8,128)(2,1)S(1)} %copy-done), kind=kOutput, calls=%fused_computation.14 | convolution fusion | flops 4433379328 | bytes 27267072 | tf_op jit(solution)/shard_map/dot_general | solution.py:112
  197.8 2.0 copy-done.36
  199.8 6.0 convolution_convert_fusion.1
  206.5 44.0 %reduce-scatter.4.cloned.1.call-done = bf16[512,1024]{1,0:T(8,128)(2,1)} async-done(((bf16[2048,1024]{1,0:T(8,128)(2,1)}), bf16[512,1024]{1,0:T(8,128)(2,1)}) %reduce-scatter.4.cloned.1.call-update) | async-done | bytes 1048592 | tf_op jit(solution)/shard_map/reduce_scatter | solution.py:118
  250.6 2.7 fusion.39
  254.6 2.0 fusion.38
  259.6 34.2 %all-gather.24.cloned.1.call-done = bf16[2048,1024]{1,0:T(8,128)(2,1)} async-done(((bf16[512,1024]{1,0:T(8,128)(2,1)}), bf16[2048,1024]{1,0:T(8,128)(2,1)}) %all-gather.24.cloned.1.call-update) | async-done | bytes 4194320 | tf_op jit(solution)/shard_map/all_gather | solution.py:115
  293.8 13.3 %fusion.34 = (bf16[1024]{0:T(1024)(128)(2,1)S(1)}, bf16[2048,1024]{1,0:T(8,128)(2,1)S(1)}) fusion(f32[2048,1024]{1,0:T(8,128)} %get-tuple-element.38, f32[2048,1024]{1,0:T(8,128)} %get-tuple-element.62, f32[1024]{0:T(1024)S(1)} %dynamic-slice_convert_fusion, bf16[2048,1024]{1,0:T(8,128)(2,1)} %all-gather.24.cloned.1.call-done, bf16[1024,1024]{1,0:T(8,128)(2,1)} %param.31), kind=kOutput, calls=%fused_computation.96 | convolution fusion | flops 4328520704 | bytes 27269120 | tf_op jit(solution)/shard_map/dot_general | solution.py:112
  307.1 1.9 copy-done.37
  309.0 6.0 convolution_convert_fusion
  315.1 44.7 %reduce-scatter.6.cloned.1.call-done = bf16[512,1024]{1,0:T(8,128)(2,1)} async-done(((bf16[2048,1024]{1,0:T(8,128)(2,1)}), bf16[512,1024]{1,0:T(8,128)(2,1)}) %reduce-scatter.6.cloned.1.call-update) | async-done | bytes 1048592 | tf_op jit(solution)/shard_map/reduce_scatter | solution.py:118
  359.8 3.7 multiply_reduce_fusion.2
  366.4 2.3 convolution_convert_fusion.8
  368.6 1.5 copy.80
  370.1 11.4 %multiply_reduce_fusion = (f32[16,512]{1,0:T(8,128)S(1)}, f32[16,512,512]{1,2,0:T(8,128)}) fusion(f32[16,512,512]{1,2,0:T(8,128)} %get-tuple-element.59, f32[16,512]{1,0:T(8,128)S(1)} %log_add_fusion, bf16[512,16,64]{0,2,1:T(8,128)(2,1)S(1)} %bitcast.101, bf16[512,16,64]{0,2,1:T(8,128)(2,1)} %bitcast.104), kind=kOutput, calls=%fused_computation.1 | convolution fusion | flops 549445632 | bytes 35717120 | tf_op jit(solution)/shard_map/qhd,khd->hqk/dot_general | solution.py:53
  381.5 12.0 %multiply_convert_fusion = bf16[16,512,512]{1,2,0:T(8,128)(2,1)S(1)} fusion(f32[16,512,512]{1,2,0:T(8,128)} %get-tuple-element.64, f32[16,512,512]{1,2,0:T(8,128)} %get-tuple-element.59, f32[16,512]{1,0:T(8,128)S(1)} %get-tuple-element.63, f32[16,512]{1,0:T(8,128)S(1)} %log_add_fusion), kind=kLoop, calls=%fused_computation | loop fusion | flops 16777216 | bytes 42008576 | tf_op jit(solution)/shard_map/convert_element_type | solution.py:57
  393.5 1.5 bitcast_reduce_fusion.1
  395.1 2.6 multiply_convert_fusion.2
  397.7 9.0 bitcast_reduce_fusion
  412.3 3.8 pad_maximum_fusion
  416.5 8.2 convolution_convert_fusion.2
  424.7 4.8 convolution_convert_fusion.3
  429.4 2.5 pad_maximum_fusion.1
  432.0 55.7 %reduce-scatter.8.cloned.1.call-done = bf16[1024,1024]{1,0:T(8,128)(2,1)} async-done(((bf16[4096,1024]{1,0:T(8,128)(2,1)}), bf16[1024,1024]{1,0:T(8,128)(2,1)}) %reduce-scatter.8.cloned.1.call-update) | async-done | bytes 2097168 | tf_op jit(solution)/shard_map/reduce_scatter | solution.py:118
  487.8 160.6 %all-reduce.2.cloned.1.call-done = bf16[2048,1024]{1,0:T(8,128)(2,1)} async-done(((bf16[2048,1024]{1,0:T(8,128)(2,1)}), bf16[2048,1024]{1,0:T(8,128)(2,1)}) %all-reduce.2.cloned.1.call-update) | async-done | bytes 4194320 | tf_op jit(solution)/shard_map/psum | solution.py:170
  648.4 6.8 fusion.41
  660.8 2.6 fusion.42
  663.8 49.0 %all-gather.2 = bf16[32,11,1024]{2,1,0:T(8,128)(2,1)S(1)} all-gather(bf16[1,11,1024]{2,1,0:T(8,128)(2,1)S(1)} %bitcast.117), channel_id=3, replica_groups=mesh['dp'=8,'seq'=4] {'dp','seq'}, dimensions={0}, use_global_device_ids=true | all-gather | bytes 743424 | tf_op jit(solution)/shard_map/all_gather | solution.py:220
  716.7 165.5 %all-gather.26.cloned.1.call-done = bf16[8192,1024]{1,0:T(8,128)(2,1)} async-done(((bf16[1024,1024]{1,0:T(8,128)(2,1)}), bf16[8192,1024]{1,0:T(8,128)(2,1)}) %all-gather.26.cloned.1.call-update) | async-done | bytes 16777232 | tf_op jit(solution)/shard_map/all_gather | solution.py:199
  882.2 10.8 %reduce_sum.264 = bf16[1024,1024]{1,0:T(8,128)(2,1)} reduce(bf16[8,1024,1024]{2,1,0:T(8,128)(2,1)} %bitcast.96, bf16[]{:T(256)} %constant.103.clone.1), dimensions={0}, to_apply=%region_14.15 | reduce | flops 7340032 | bytes 18874370 | tf_op jit(solution)/shard_map/reduce_sum | solution.py:199
  893.0 3.7 fusion.43
  (155 shorter events, 34.5 us)
Async XLA Ops:
  7.2 164.9 %copy-start = (bf16[1024,1024]{1,0:T(8,128)(2,1)S(1)}, bf16[1024,1024]{1,0:T(8,128)(2,1)}, u32[]{:S(2)}) copy-start(bf16[1024,1024]{1,0:T(8,128)(2,1)} %param.30) | copy-start | bytes 6291460
  7.2 29.7 %copy-start.27 = (bf16[1024]{0:T(1024)(128)(2,1)S(1)}, bf16[1024]{0:T(1024)(128)(2,1)}, u32[]{:S(2)}) copy-start(bf16[1024]{0:T(1024)(128)(2,1)} %param.35) | copy-start | bytes 6148
  7.2 27.7 %all-gather.12.cloned.1.call-start = ((), (), s32[]{:S(2)}) async-start(), calls=%async_computation.3 | async-start | bytes 2621440 | tf_op jit(solution)/shard_map/all_gather | solution.py:115
  7.9 51.1 %all-gather.16.cloned.1.call-start = ((), (), s32[]{:S(2)}) async-start(), calls=%async_computation.5 | async-start | bytes 2621440 | tf_op jit(solution)/shard_map/all_gather | solution.py:115
  8.7 74.5 %all-gather.18.cloned.1.call-start = ((), (), s32[]{:S(2)}) async-start(), calls=%async_computation.6 | async-start | bytes 2621440 | tf_op jit(solution)/shard_map/all_gather | solution.py:115
  9.4 97.8 %all-gather.14.cloned.1.call-start = ((), (), s32[]{:S(2)}) async-start(), calls=%async_computation.4 | async-start | bytes 2621440 | tf_op jit(solution)/shard_map/all_gather | solution.py:115
  10.0 121.2 %all-gather.20.cloned.1.call-start = ((), (), s32[]{:S(2)}) async-start(), calls=%async_computation.7 | async-start | bytes 2621440 | tf_op jit(solution)/shard_map/all_gather | solution.py:115
  10.6 161.5 %all-gather.22.cloned.1.call-start = ((), (), s32[]{:S(2)}) async-start(), calls=%async_computation.8 | async-start | bytes 5242880 | tf_op jit(solution)/shard_map/all_gather | solution.py:115
  36.9 94.3 %copy-start.24 = (f32[1024]{0:T(1024)}, f32[1024]{0:T(1024)S(1)}, u32[]{:S(2)}) copy-start(f32[1024]{0:T(1024)S(1)} %convert_add_fusion.2) | copy-start | bytes 12292
  88.9 9.2 %copy-start.5 = (bf16[512,1024]{0,1:T(8,128)(2,1)}, bf16[512,1024]{0,1:T(8,128)(2,1)S(1)}, u32[]{:S(2)}) copy-start(bf16[512,1024]{0,1:T(8,128)(2,1)S(1)} %copy.78) | copy-start | bytes 3145732
  112.9 9.4 %copy-start.10 = (bf16[512,1024]{0,1:T(8,128)(2,1)}, bf16[512,1024]{0,1:T(8,128)(2,1)S(1)}, u32[]{:S(2)}) copy-start(bf16[512,1024]{0,1:T(8,128)(2,1)S(1)} %copy.76) | copy-start | bytes 3145732
  134.8 1.3 copy-start.1
  137.5 113.1 %reduce-scatter.4.cloned.1.call-start = ((), (), s32[]{:S(2)}) async-start(), calls=%async_computation.9 | async-start | bytes 5242880 | tf_op jit(solution)/shard_map/reduce_scatter | solution.py:118
  172.1 27.7 %copy-start.32 = (bf16[1024,1024]{1,0:T(8,128)(2,1)S(1)}, bf16[1024,1024]{1,0:T(8,128)(2,1)}, u32[]{:S(2)}) copy-start(bf16[1024,1024]{1,0:T(8,128)(2,1)} %param.31) | copy-start | bytes 6291460
  197.8 2.0 copy-start.36
  205.8 47.8 %copy-start.11 = (bf16[512,1024]{1,0:T(8,128)(2,1)S(1)}, bf16[512,1024]{1,0:T(8,128)(2,1)}, u32[]{:S(2)}) copy-start(bf16[512,1024]{1,0:T(8,128)(2,1)} %param.24) | copy-start | bytes 3145732
  205.9 87.9 %all-gather.24.cloned.1.call-start = ((), (), s32[]{:S(2)}) async-start(), calls=%async_computation.10 | async-start | bytes 5242880 | tf_op jit(solution)/shard_map/all_gather | solution.py:115
  256.6 1.3 copy-start.3
  259.2 100.6 %reduce-scatter.6.cloned.1.call-start = ((), (), s32[]{:S(2)}) async-start(), calls=%async_computation.11 | async-start | bytes 5242880 | tf_op jit(solution)/shard_map/reduce_scatter | solution.py:118
  307.1 1.9 copy-start.37
  315.0 172.7 %reduce-scatter.8.cloned.1.call-start = ((), (), s32[]{:S(2)}) async-start(), calls=%async_computation.12 | async-start | bytes 10485760 | tf_op jit(solution)/shard_map/reduce_scatter | solution.py:118
  359.8 3.7 copy-start.2
  359.8 3.8 copy-start.4
  359.8 4.0 copy-start.12
  363.8 2.6 copy-start.15
  364.7 1.3 copy-start.8
  365.0 1.4 copy-start.18
  381.5 12.0 %copy-start.6 = (bf16[512,1024]{0,1:T(8,128)(2,1)S(1)}, bf16[512,1024]{0,1:T(8,128)(2,1)}, u32[]{:S(2)}) copy-start(bf16[512,1024]{0,1:T(8,128)(2,1)} %copy-done.5) | copy-start | bytes 3145732
  393.5 1.5 copy-start.7
  395.1 12.9 %copy-start.13 = (bf16[16,64,512]{2,1,0:T(8,128)(2,1)}, bf16[16,64,512]{2,1,0:T(8,128)(2,1)S(1)}, u32[]{:S(2)}) copy-start(bf16[16,64,512]{2,1,0:T(8,128)(2,1)S(1)} %get-tuple-element.67) | copy-start | bytes 3145732
  397.7 12.0 %copy-start.16 = (bf16[16,64,512]{2,1,0:T(8,128)(2,1)}, bf16[16,64,512]{2,1,0:T(8,128)(2,1)S(1)}, u32[]{:S(2)}) copy-start(bf16[16,64,512]{2,1,0:T(8,128)(2,1)S(1)} %multiply_convert_fusion.2) | copy-start | bytes 3145732
  397.7 9.0 copy-start.19
  397.7 9.0 copy-start.21
  406.7 4.3 copy-start.22
  406.7 1.6 copy-start.20
  406.7 1.6 copy-start.25
  416.2 232.2 %all-reduce.2.cloned.1.call-start = ((), (), s32[]{:S(2)}) async-start(), calls=%async_computation.13 | async-start | bytes 8388608 | tf_op jit(solution)/shard_map/psum | solution.py:170
  416.4 8.2 copy-start.31
  416.4 8.2 copy-start.38
  431.9 450.3 %all-gather.26.cloned.1.call-start = ((), (), s32[]{:S(2)}) async-start(), calls=%async_computation.14 | async-start | bytes 18874368 | tf_op jit(solution)/shard_map/all_gather | solution.py:199
  487.8 167.4 %copy-start.14 = (bf16[16,64,512]{2,1,0:T(8,128)(2,1)S(1)}, bf16[16,64,512]{2,1,0:T(8,128)(2,1)}, u32[]{:S(2)}) copy-start(bf16[16,64,512]{2,1,0:T(8,128)(2,1)} %copy-done.13) | copy-start | bytes 3145732
  648.4 6.8 copy-start.33
  655.2 1.3 copy-start.17
  655.2 2.3 copy-start.34
  657.6 2.0 copy-start.9
  657.6 2.4 copy-start.23
  657.6 3.2 copy-start.35
  660.8 2.9 copy-start.26
  (3 other events, 2.1 us)
Sparse Core Ops, SparseCore 0:
  9.6 25.2 all-gather.11
  36.5 22.5 all-gather.15
  60.6 22.5 all-gather.17
  84.6 22.5 all-gather.13
  108.6 22.5 all-gather.19
  137.6 34.4 all-gather.21
  206.0 44.5 reduce-scatter.3
  259.3 34.4 all-gather.23
  315.1 44.5 reduce-scatter.5
  416.3 71.3 reduce-scatter.7
  492.0 156.3 all-reduce.1
  650.4 231.7 all-gather.25
